TPU v7x, 128 devices: a whole 4x4x4 slice. The times are simulated.
128 devices in a mesh: shard: 32 (over y, z, core), rep: 4 (over x).
Axes of the slice: x: 4, y: 4, z: 4, core: 2. Of those that a mesh axis runs over, the one named last changes fastest.
Arguments:
- feats: bfloat16 [32768, 768], P('shard'), may hold values from -6 to 6
- bases: bfloat16 [4, 768, 1024], P(None, None, 'rep'), may hold values from -0.21875 to 0.21875
- coef: bfloat16 [5, 4], replicated, may hold values from -2 to 2
- root_weight: bfloat16 [768, 1024], P(None, 'rep'), may hold values from -0.21875 to 0.21875
- slot_block: int32 [32, 32, 2], P('shard'), may hold values from 0 to 7
- recv_rel: int32 [32, 32, 2], P('shard'), may hold values from 0 to 4
- tile_slot: int32 [32, 256], P('shard'), may hold values from 0 to 63, as said below
- tile_dst: int32 [32, 256], P('shard'), may hold values from 0 to 7
- tile_adj: bfloat16 [32, 256, 128, 128], P('shard'), may hold values from 0 to 0.049804688
- d_out: bfloat16 [32768, 1024], P('shard', 'rep'), may hold values from -6 to 6
Outputs:
- output: bfloat16 [32768, 1024], P('shard', 'rep')
- grad_feats: bfloat16 [32768, 768], P(('shard', 'rep'))
- grad_bases: float32 [4, 768, 1024], P(None, 'shard', 'rep')
- grad_root: float32 [768, 1024], P('shard', 'rep')
- grad_coef: float32 [5, 4], replicated
Inputs may be any that keep to these rules, and one draw needn't show every extreme that they name: `tile_slot`: in each row (one destination device) every one of the 64 slots is named by at least one tile.
All inputs are finite; a program needn't handle non-finite values.
Results may differ from a plain program's by a relative error of at most 0.0062.
Values may be sent and summed in bfloat16 or wider, within the bound.
No kernel may reach another device: no remote copies, remote signals or barrier semaphores. Data moves between devices by JAX's collectives and lax.ppermute only.
A program may use at most 192 MiB of HBM per device.

v0:
```python
import jax
import jax.numpy as jnp
from jax import lax
from jax.sharding import PartitionSpec as P

BLK = 128
highest = lax.Precision.HIGHEST


def project_slots(source, weights):
    return jnp.einsum("snc,sco->sno", source, weights, preferred_element_type=jnp.float32).astype(
        jnp.bfloat16
    )


def body(
    feats, bases, coef, root_weight, slot_block, recv_rel, tile_slot, tile_dst, tile_adj, d_out
):
    shards = lax.axis_size("shard")
    nblocks = feats.shape[0] // BLK
    width_in = feats.shape[1]
    width_out = root_weight.shape[1]
    relations = coef.shape[0]
    capacity = slot_block.shape[2]
    slot_count = shards * capacity
    rel_weights = (
        jnp.dot(coef, bases.reshape(bases.shape[0], -1), preferred_element_type=jnp.float32)
        .astype(jnp.bfloat16)
        .reshape(relations, width_in, width_out)
    )
    feat_blocks = feats.reshape(nblocks, BLK, width_in)
    send_block = slot_block[0]
    local_rel = recv_rel[0]
    owner_rel = lax.all_to_all(local_rel, "shard", split_axis=0, concat_axis=0, tiled=True)
    tile_ids = tile_slot[0]
    dest_ids = tile_dst[0]
    adjacency = tile_adj[0]
    root_term = jnp.dot(feats, root_weight, preferred_element_type=jnp.float32)
    slot_weights = rel_weights[local_rel.reshape(-1)]
    outgoing = feat_blocks[send_block]
    incoming = lax.all_to_all(outgoing, "shard", split_axis=0, concat_axis=0, tiled=True)
    slot_msgs = project_slots(incoming.reshape(slot_count, BLK, width_in), slot_weights)
    tile_msgs = slot_msgs[tile_ids]
    weighted = jnp.einsum("tij,tjo->tio", adjacency, tile_msgs, preferred_element_type=jnp.float32)
    dst_onehot = (dest_ids[:, None] == jnp.arange(nblocks)[None, :]).astype(jnp.float32)
    neighbor_sum = jnp.einsum("tb,tio->bio", dst_onehot, weighted, precision=highest).reshape(
        -1, width_out
    )
    output = (neighbor_sum + root_term).astype(jnp.bfloat16)
    grad_rows = d_out.reshape(nblocks, BLK, width_out)[dest_ids]
    tile_grads = jnp.einsum(
        "tji,tjo->tio", adjacency, grad_rows, preferred_element_type=jnp.float32
    )
    slot_onehot = (tile_ids[:, None] == jnp.arange(slot_count)[None, :]).astype(jnp.float32)
    slot_grads = jnp.einsum("ts,tio->sio", slot_onehot, tile_grads, precision=highest).astype(
        jnp.bfloat16
    )
    slot_grads = slot_grads.reshape(shards, capacity, BLK, width_out)
    returned = lax.all_to_all(slot_grads, "shard", split_axis=0, concat_axis=0, tiled=True)
    owner_key = (owner_rel * nblocks + send_block).reshape(-1)
    owner_onehot = (owner_key[:, None] == jnp.arange(relations * nblocks)[None, :]).astype(
        jnp.bfloat16
    )
    source_grads = jnp.einsum(
        "sk,sio->kio",
        owner_onehot,
        returned.reshape(slot_count, BLK, width_out),
        preferred_element_type=jnp.float32,
    )
    source_grads = source_grads.astype(jnp.bfloat16).reshape(relations, nblocks * BLK, width_out)
    through_rel = jnp.einsum(
        "rno,rco->nc", source_grads, rel_weights, preferred_element_type=jnp.float32
    )
    feature_sum = lax.psum_scatter(
        through_rel + jnp.dot(d_out, root_weight.T, preferred_element_type=jnp.float32),
        "rep",
        scatter_dimension=0,
        tiled=True,
    )
    grad_feats = feature_sum.astype(jnp.bfloat16)
    relation_grads = jnp.einsum(
        "nc,rno->cro", feats, source_grads, preferred_element_type=jnp.float32
    )
    root_grad = jnp.dot(feats.T, d_out, preferred_element_type=jnp.float32)
    stacked = jnp.concatenate([relation_grads, root_grad[:, None, :]], axis=1)
    reduced = lax.psum_scatter(stacked, "shard", scatter_dimension=0, tiled=True)
    grad_bases = jnp.einsum(
        "rb,iro->bio", coef.astype(jnp.float32), reduced[:, :relations], precision=highest
    )
    grad_root = reduced[:, relations]
    row_count = reduced.shape[0]
    base_rows = lax.dynamic_slice_in_dim(bases, lax.axis_index("shard") * row_count, row_count, 1)
    partial_coef = jnp.einsum(
        "iro,bio->rb", reduced[:, :relations], base_rows.astype(jnp.float32), precision=highest
    )
    grad_coef = lax.psum(partial_coef, ("shard", "rep"))
    return (output, grad_feats, grad_bases, grad_root, grad_coef)


def solution(mesh):
    placed = (
        P("shard", None),
        P(None, None, "rep"),
        P(),
        P(None, "rep"),
        P("shard", None, None),
        P("shard", None, None),
        P("shard", None),
        P("shard", None),
        P("shard", None, None, None),
        P("shard", "rep"),
    )
    return jax.shard_map(
        body,
        mesh=mesh,
        in_specs=placed,
        out_specs=(
            P("shard", "rep"),
            P(("shard", "rep"), None),
            P(None, "shard", "rep"),
            P("shard", "rep"),
            P(),
        ),
        check_vma=False,
    )
```

profile of v0, /device:TPU:1, one launch (start us, length us, event | category | flops | bytes accessed | tf_op | source)
XLA Modules:
  0.0 624.1 jit_solution(11586295730918086103)
XLA Ops:
  8.7 9.6 %all-to-all-start.1 = ((s32[32,1,2]{2,1,0:T(1,128)}), s32[32,1,2]{2,1,0:T(1,128)S(1)}, u32[]{:S(2)}, u32[]{:S(2)}) async-start(s32[32,1,2]{2,1,0:T(1,128)} %copy.60), calls=%async_computation.1 | async-start | bytes 32768 | tf_op jit(solution)/shard_map/all_to_all | solution.py:34
  19.0 10.8 %gather_fusion.3 = bf16[256,128,256]{2,1,0:T(8,128)(2,1)} fusion(bf16[8,128,256]{2,1,0:T(8,128)(2,1)} %bitcast.87, s32[1024]{0:T(1024)S(1)} %pad_clamp_fusion), kind=kCustom, calls=%fused_computation.3 | custom fusion | bytes 33555456 | tf_op jit(solution)/shard_map/gather | solution.py:50
  29.8 20.1 %convolution_bitcast_fusion = f32[256,128,256]{1,2,0:T(8,128)} fusion(bf16[256,128,256]{2,1,0:T(8,128)(2,1)} %gather_fusion.3, bf16[1,256,128,128]{3,2,1,0:T(8,128)(2,1)} %param.18), kind=kOutput, calls=%fused_computation.5 | convolution fusion | flops 2147483648 | bytes 58720256 | tf_op jit(solution)/shard_map/tji,tjo->tio/dot_general | solution.py:51
  49.9 33.4 %copy.63 = f32[256,128,256]{2,0,1:T(8,128)} copy(f32[256,128,256]{1,2,0:T(8,128)} %convolution_bitcast_fusion) | data formatting | bytes 67108864 | tf_op jit(solution)/shard_map/tji,tjo->tio/dot_general | solution.py:51
  83.3 19.2 %convolution_convert_fusion.1 = bf16[64,128,256]{2,0,1:T(8,128)(2,1)} fusion(f32[256,128,256]{2,0,1:T(8,128)} %copy.63, s32[256]{0:T(256)S(1)} %bitcast.99), kind=kOutput, calls=%fused_computation.11 | convolution fusion | flops 6444564480 | bytes 37749760 | tf_op jit(solution)/shard_map/ts,tio->sio/dot_general | solution.py:55
  102.4 7.2 %reshape.172 = bf16[32,2,128,256]{3,1,0,2:T(2,128)(2,1)} reshape(bf16[64,128,256]{2,0,1:T(8,128)(2,1)} %convolution_convert_fusion.1) | data formatting | bytes 8388608 | tf_op jit(solution)/shard_map/reshape | solution.py:58
  109.7 8.5 %copy.64 = bf16[32,2,128,256]{3,1,2,0:T(2,128)(2,1)} copy(bf16[32,2,128,256]{3,1,0,2:T(2,128)(2,1)} %reshape.172) | data formatting | bytes 8388608 | tf_op jit(solution)/shard_map/reshape | solution.py:58
  118.2 7.6 %all-to-all-start.2 = ((bf16[32,2,128,256]{3,1,2,0:T(2,128)(2,1)}), bf16[32,2,128,256]{3,1,2,0:T(2,128)(2,1)}, u32[]{:S(2)}, u32[]{:S(2)}) async-start(bf16[32,2,128,256]{3,1,2,0:T(2,128)(2,1)} %copy.64), calls=%async_computation.2 | async-start | bytes 8388608 | tf_op jit(solution)/shard_map/all_to_all | solution.py:59
  125.8 11.4 %reduce-scatter.5.cloned.1.call-start = ((), (), s32[]{:S(2)}) async-start(), calls=%async_computation.6 | async-start | bytes 6488064 | tf_op jit(solution)/shard_map/reduce_scatter | solution.py:86
  138.2 39.7 %all-to-all-done.2 = bf16[32,2,128,256]{3,1,2,0:T(2,128)(2,1)} async-done(((bf16[32,2,128,256]{3,1,2,0:T(2,128)(2,1)}), bf16[32,2,128,256]{3,1,2,0:T(2,128)(2,1)}, u32[]{:S(2)}, u32[]{:S(2)}) %all-to-all-start.2) | async-done | bytes 4194336 | tf_op jit(solution)/shard_map/all_to_all | solution.py:59
  178.0 8.9 %copy.65 = bf16[32,2,128,256]{3,1,0,2:T(2,128)(2,1)} copy(bf16[32,2,128,256]{3,1,2,0:T(2,128)(2,1)} %all-to-all-done.2) | data formatting | bytes 8388608 | tf_op jit(solution)/shard_map/all_to_all | solution.py:59
  186.9 7.2 %reshape.173 = bf16[64,128,256]{2,0,1:T(8,128)(2,1)} reshape(bf16[32,2,128,256]{3,1,0,2:T(2,128)(2,1)} %copy.65) | data formatting | bytes 8388608 | tf_op jit(solution)/shard_map/reshape | solution.py:67
  202.6 6.3 %copy.69 = f32[768,6,256]{2,1,0:T(8,128)} copy(f32[768,6,256]{0,2,1:T(8,128)} %pad_maximum_fusion) | data formatting | bytes 9437184 | tf_op jit(solution)/shard_map/concatenate | solution.py:85
  209.1 7.2 %gather_fusion = bf16[64,128,768]{2,1,0:T(8,128)(2,1)} fusion(bf16[8,128,768]{2,1,0:T(8,128)(2,1)S(1)} %bitcast.86, s32[1024]{0:T(1024)S(1)} %pad_clamp_fusion.3), kind=kCustom, calls=%fused_computation | custom fusion | bytes 25166080 | tf_op jit(solution)/shard_map/gather | solution.py:40
  216.3 7.3 %all-to-all-start = ((bf16[32,2,128,768]{3,2,1,0:T(8,128)(2,1)}), bf16[32,2,128,768]{3,2,1,0:T(8,128)(2,1)}, u32[]{:S(2)}, u32[]{:S(2)}) async-start(bf16[32,2,128,768]{3,2,1,0:T(8,128)(2,1)} %bitcast.90), calls=%async_computation | async-start | bytes 25165824 | tf_op jit(solution)/shard_map/all_to_all | solution.py:41
  235.0 11.0 %gather_fusion.1 = bf16[64,768,256]{2,1,0:T(8,128)(2,1)} fusion(bf16[5,768,256]{2,1,0:T(8,128)(2,1)S(1)} %bitcast.89, s32[1024]{0:T(1024)S(1)} %pad_clamp_fusion.2), kind=kCustom, calls=%fused_computation.1 | custom fusion | bytes 50331904 | tf_op jit(solution)/shard_map/gather | solution.py:39
  246.8 159.7 %reduce-scatter.5.cloned.1.call-done = f32[24,6,256]{2,1,0:T(8,128)} async-done(((f32[768,6,256]{2,1,0:T(8,128)}), f32[24,6,256]{2,1,0:T(8,128)}) %reduce-scatter.5.cloned.1.call-update) | async-done | bytes 147472 | tf_op jit(solution)/shard_map/reduce_scatter | solution.py:86
  407.7 40.2 %reduce-scatter.3.cloned.1.call-done = f32[256,768]{1,0:T(8,128)} async-done(((f32[1024,768]{1,0:T(8,128)}), f32[256,768]{1,0:T(8,128)}) %reduce-scatter.3.cloned.1.call-update) | async-done | bytes 786448 | tf_op jit(solution)/shard_map/reduce_scatter | solution.py:74
  449.9 64.9 %psum.7 = f32[5,4]{0,1:T(4,128)} all-reduce(f32[5,4]{0,1:T(4,128)S(1)} %convolution_bitcast_fusion.5), channel_id=1, replica_groups=mesh['shard'=32,'rep'=4] {'shard','rep'}, use_global_device_ids=true, to_apply=%region_2.0 | all-reduce | flops 20 | bytes 160 | tf_op jit(solution)/shard_map/psum | solution.py:96
  518.1 15.7 %convolution_convert_fusion.2 = bf16[64,128,256]{2,1,0:T(8,128)(2,1)} fusion(bf16[64,128,768]{2,1,0:T(8,128)(2,1)} %bitcast.5, bf16[64,768,256]{2,1,0:T(8,128)(2,1)} %gather_fusion.1), kind=kOutput, calls=%fused_computation.12 | convolution fusion | flops 3223322624 | bytes 41943040 | tf_op jit(solution)/shard_map/snc,sco->sno/dot_general | solution.py:11
  533.9 12.0 %gather_fusion.2 = bf16[256,128,256]{2,1,0:T(8,128)(2,1)} fusion(bf16[64,128,256]{2,1,0:T(8,128)(2,1)} %convolution_convert_fusion.2, s32[1024]{0:T(1024)S(1)} %pad_clamp_fusion.1), kind=kCustom, calls=%fused_computation.2 | custom fusion | bytes 33555456 | tf_op jit(solution)/shard_map/gather | solution.py:43
  545.9 20.1 %convolution_bitcast_fusion.1 = f32[256,128,256]{1,2,0:T(8,128)} fusion(bf16[256,128,256]{2,1,0:T(8,128)(2,1)} %gather_fusion.2, bf16[1,256,128,128]{3,2,1,0:T(8,128)(2,1)} %param.18), kind=kOutput, calls=%fused_computation.6 | convolution fusion | flops 2147483648 | bytes 58720256 | tf_op jit(solution)/shard_map/tij,tjo->tio/dot_general | solution.py:44
  566.0 33.4 %copy.58 = f32[256,128,256]{2,0,1:T(8,128)} copy(f32[256,128,256]{1,2,0:T(8,128)} %convolution_bitcast_fusion.1) | data formatting | bytes 67108864 | tf_op jit(solution)/shard_map/tij,tjo->tio/dot_general | solution.py:44
  599.4 15.8 %fusion.14 = f32[8,128,256]{2,0,1:T(8,128)S(1)} fusion(f32[256,128,256]{2,0,1:T(8,128)} %copy.58, s32[256]{0:T(256)S(1)} %bitcast.98), kind=kOutput, calls=%fused_computation.35 | convolution fusion | flops 805308416 | bytes 34604032 | tf_op jit(solution)/shard_map/tb,tio->bio/dot_general | solution.py:46
  (70 shorter events, 32.2 us)
Async XLA Ops:
  7.2 130.3 %copy-start = (bf16[1024,768]{1,0:T(8,128)(2,1)S(1)}, bf16[1024,768]{1,0:T(8,128)(2,1)}, u32[]{:S(2)}) copy-start(bf16[1024,768]{1,0:T(8,128)(2,1)} %param.10) | copy-start | bytes 4718596
  8.7 109.5 %all-to-all-start.1 = ((s32[32,1,2]{2,1,0:T(1,128)}), s32[32,1,2]{2,1,0:T(1,128)S(1)}, u32[]{:S(2)}, u32[]{:S(2)}) async-start(s32[32,1,2]{2,1,0:T(1,128)} %copy.60), calls=%async_computation.1 | async-start | bytes 32768 | tf_op jit(solution)/shard_map/all_to_all | solution.py:34
  49.9 33.4 %copy-start.9 = (s32[1,256]{1,0:T(1,128)S(1)}, s32[1,256]{1,0:T(1,128)}, u32[]{:S(2)}) copy-start(s32[1,256]{1,0:T(1,128)} %param.16) | copy-start | bytes 3076
  118.2 19.0 %copy-start.11 = (s32[1,32,2]{1,2,0:T(2,128)S(1)}, s32[1,32,2]{1,2,0:T(2,128)}, u32[]{:S(2)}) copy-start(s32[1,32,2]{1,2,0:T(2,128)} %param.14) | copy-start | bytes 772
  118.2 19.2 %copy-start.1 = (bf16[1024,256]{1,0:T(8,128)(2,1)S(1)}, bf16[1024,256]{1,0:T(8,128)(2,1)}, u32[]{:S(2)}) copy-start(bf16[1024,256]{1,0:T(8,128)(2,1)} %param.19) | copy-start | bytes 1572868
  118.2 59.8 %all-to-all-start.2 = ((bf16[32,2,128,256]{3,1,2,0:T(2,128)(2,1)}), bf16[32,2,128,256]{3,1,2,0:T(2,128)(2,1)}, u32[]{:S(2)}, u32[]{:S(2)}) async-start(bf16[32,2,128,256]{3,1,2,0:T(2,128)(2,1)} %copy.64), calls=%async_computation.2 | async-start | bytes 8388608 | tf_op jit(solution)/shard_map/all_to_all | solution.py:59
  125.8 280.7 %reduce-scatter.5.cloned.1.call-start = ((), (), s32[]{:S(2)}) async-start(), calls=%async_computation.6 | async-start | bytes 6488064 | tf_op jit(solution)/shard_map/reduce_scatter | solution.py:86
  197.7 2.3 copy-start.4
  216.3 10.0 %copy-start.12 = (bf16[5,4]{0,1:T(4,128)(2,1)S(1)}, bf16[5,4]{0,1:T(4,128)(2,1)}, u32[]{:S(2)}) copy-start(bf16[5,4]{0,1:T(4,128)(2,1)} %param.12) | copy-start | bytes 124
  216.3 301.8 %all-to-all-start = ((bf16[32,2,128,768]{3,2,1,0:T(8,128)(2,1)}), bf16[32,2,128,768]{3,2,1,0:T(8,128)(2,1)}, u32[]{:S(2)}, u32[]{:S(2)}) async-start(bf16[32,2,128,768]{3,2,1,0:T(8,128)(2,1)} %bitcast.90), calls=%async_computation | async-start | bytes 25165824 | tf_op jit(solution)/shard_map/all_to_all | solution.py:41
  223.6 224.3 %reduce-scatter.3.cloned.1.call-start = ((), (), s32[]{:S(2)}) async-start(), calls=%async_computation.5 | async-start | bytes 3932160 | tf_op jit(solution)/shard_map/reduce_scatter | solution.py:74
  226.4 1.8 copy-start.5
  228.2 2.3 copy-start.2
  228.2 2.2 copy-start.6
  232.8 2.2 copy-start.3
  235.0 11.0 %copy-start.10 = (s32[1,256]{1,0:T(1,128)S(1)}, s32[1,256]{1,0:T(1,128)}, u32[]{:S(2)}) copy-start(s32[1,256]{1,0:T(1,128)} %param.16) | copy-start | bytes 3076
  235.0 279.8 %copy-start.13 = (bf16[5,4]{0,1:T(4,128)(2,1)S(1)}, bf16[5,4]{0,1:T(4,128)(2,1)}, u32[]{:S(2)}) copy-start(bf16[5,4]{0,1:T(4,128)(2,1)} %param.12) | copy-start | bytes 124
  566.0 33.4 %copy-start.8 = (s32[1,256]{1,0:T(1,128)S(1)}, s32[1,256]{1,0:T(1,128)}, u32[]{:S(2)}) copy-start(s32[1,256]{1,0:T(1,128)} %param.17) | copy-start | bytes 3076
  599.4 16.1 %copy-start.7 = (bf16[768,256]{1,0:T(8,128)(2,1)S(1)}, bf16[768,256]{1,0:T(8,128)(2,1)}, u32[]{:S(2)}) copy-start(bf16[768,256]{1,0:T(8,128)(2,1)} %param.13) | copy-start | bytes 1179652
Sparse Core Ops, SparseCore 0:
  209.0 197.4 reduce-scatter.4
  409.0 38.8 reduce-scatter.2
where the time goes:
time: 635 us; the launch traced here: 624 us
  waiting for transfers between devices  240 us (38%)
  local copies, waits for them, and re-layouts  157 us (25%)
  matrix products  106 us (17%)
  blocking collectives  64.9 us (10%)
  starting transfers between devices  35.9 us (6%)
  between operations  14.7 us (2%)
    reduce_scatter x1, waiting for transfers between devices, body(): lax.psum_scatter(stacked, 'shard', scatter_dimension=0, tiled=True)  160 us
    psum x1, blocking collectives, body(): grad_coef = lax.psum(partial_coef, ('shard', 'rep'))  64.9 us
    reduce_scatter x1, waiting for transfers between devices, body(): lax.psum_scatter(through_rel + jnp.dot(d_out, root_weight.T, preferred_el...  40.2 us
    all_to_all x1, waiting for transfers between devices, body(): lax.all_to_all(slot_grads, 'shard', split_axis=0, concat_axis=0, tiled=True)  39.7 us
    dot_general x1, local copies, waits for them, and re-layouts, body(): jnp.einsum('tij,tjo->tio', adjacency, tile_msgs, preferred_element_type=j...  33.4 us
    dot_general x1, local copies, waits for them, and re-layouts, body(): jnp.einsum('tji,tjo->tio', adjacency, grad_rows, preferred_element_type=j...  33.4 us
    dot_general x1, matrix products, body(): jnp.einsum('tij,tjo->tio', adjacency, tile_msgs, preferred_element_type=j...  20.1 us
    dot_general x1, matrix products, body(): jnp.einsum('tji,tjo->tio', adjacency, grad_rows, preferred_element_type=j...  20.1 us
  transfers between devices with their start and end apart: 5, of which 3 were waited for; matrix products, arithmetic and copies ran while one was open for 22% of the time, Pallas kernels for 0%

commit v1 on v0

--- a/solution.py
+++ b/solution.py
@@ -93,7 +93,7 @@
     partial_coef = jnp.einsum(
         "iro,bio->rb", reduced[:, :relations], base_rows.astype(jnp.float32), precision=highest
     )
-    grad_coef = lax.psum(partial_coef, ("shard", "rep"))
+    grad_coef = lax.psum(lax.psum(partial_coef, "shard"), "rep")
     return (output, grad_feats, grad_bases, grad_root, grad_coef)
 
 

time: 635 us -> 646 us (1.017)
  the two profiles are of different devices: /device:TPU:1 before, /device:TPU:0 now
where the time goes in v1:
time: 646 us; the launch traced here: 635 us
  waiting for transfers between devices  240 us (37%)
  local copies, waits for them, and re-layouts  157 us (24%)
  matrix products  106 us (16%)
  blocking collectives  76.6 us (12%)
  starting transfers between devices  34.5 us (5%)
  between operations  14.7 us (2%)
    reduce_scatter x1, waiting for transfers between devices, body(): lax.psum_scatter(stacked, 'shard', scatter_dimension=0, tiled=True)  161 us
    psum x2, blocking collectives, body(): grad_coef = lax.psum(lax.psum(partial_coef, 'shard'), 'rep')  76.6 us
    all_to_all x1, waiting for transfers between devices, body(): lax.all_to_all(slot_grads, 'shard', split_axis=0, concat_axis=0, tiled=True)  40.1 us
    reduce_scatter x1, waiting for transfers between devices, body(): lax.psum_scatter(through_rel + jnp.dot(d_out, root_weight.T, preferred_el...  38.7 us
    dot_general x1, local copies, waits for them, and re-layouts, body(): jnp.einsum('tji,tjo->tio', adjacency, grad_rows, preferred_element_type=j...  33.4 us
    dot_general x1, local copies, waits for them, and re-layouts, body(): jnp.einsum('tij,tjo->tio', adjacency, tile_msgs, preferred_element_type=j...  33.4 us
    dot_general x1, matrix products, body(): jnp.einsum('tij,tjo->tio', adjacency, tile_msgs, preferred_element_type=j...  20.1 us
    dot_general x1, matrix products, body(): jnp.einsum('tji,tjo->tio', adjacency, grad_rows, preferred_element_type=j...  20.1 us
  transfers between devices with their start and end apart: 5, of which 3 were waited for; matrix products, arithmetic and copies ran while one was open for 22% of the time, Pallas kernels for 0%

profile of v1, /device:TPU:0, one launch (start us, length us, event | category | flops | bytes accessed | tf_op | source)
XLA Modules:
  0.0 635.0 jit_solution(7494128126219569070)
XLA Ops:
  8.7 8.4 %all-to-all-start.1 = ((s32[32,1,2]{2,1,0:T(1,128)}), s32[32,1,2]{2,1,0:T(1,128)S(1)}, u32[]{:S(2)}, u32[]{:S(2)}) async-start(s32[32,1,2]{2,1,0:T(1,128)} %copy.60), calls=%async_computation.1 | async-start | bytes 32768 | tf_op jit(solution)/shard_map/all_to_all | solution.py:34
  17.8 10.8 %gather_fusion.3 = bf16[256,128,256]{2,1,0:T(8,128)(2,1)} fusion(bf16[8,128,256]{2,1,0:T(8,128)(2,1)} %bitcast.87, s32[1024]{0:T(1024)S(1)} %pad_clamp_fusion), kind=kCustom, calls=%fused_computation.3 | custom fusion | bytes 33555456 | tf_op jit(solution)/shard_map/gather | solution.py:50
  28.6 20.1 %convolution_bitcast_fusion = f32[256,128,256]{1,2,0:T(8,128)} fusion(bf16[256,128,256]{2,1,0:T(8,128)(2,1)} %gather_fusion.3, bf16[1,256,128,128]{3,2,1,0:T(8,128)(2,1)} %param.18), kind=kOutput, calls=%fused_computation.5 | convolution fusion | flops 2147483648 | bytes 58720256 | tf_op jit(solution)/shard_map/tji,tjo->tio/dot_general | solution.py:51
  48.7 33.4 %copy.63 = f32[256,128,256]{2,0,1:T(8,128)} copy(f32[256,128,256]{1,2,0:T(8,128)} %convolution_bitcast_fusion) | data formatting | bytes 67108864 | tf_op jit(solution)/shard_map/tji,tjo->tio/dot_general | solution.py:51
  82.1 19.1 %convolution_convert_fusion.1 = bf16[64,128,256]{2,0,1:T(8,128)(2,1)} fusion(f32[256,128,256]{2,0,1:T(8,128)} %copy.63, s32[256]{0:T(256)S(1)} %bitcast.99), kind=kOutput, calls=%fused_computation.11 | convolution fusion | flops 6444564480 | bytes 37749760 | tf_op jit(solution)/shard_map/ts,tio->sio/dot_general | solution.py:55
  101.3 7.3 %reshape.172 = bf16[32,2,128,256]{3,1,0,2:T(2,128)(2,1)} reshape(bf16[64,128,256]{2,0,1:T(8,128)(2,1)} %convolution_convert_fusion.1) | data formatting | bytes 8388608 | tf_op jit(solution)/shard_map/reshape | solution.py:58
  108.6 8.5 %copy.64 = bf16[32,2,128,256]{3,1,2,0:T(2,128)(2,1)} copy(bf16[32,2,128,256]{3,1,0,2:T(2,128)(2,1)} %reshape.172) | data formatting | bytes 8388608 | tf_op jit(solution)/shard_map/reshape | solution.py:58
  117.1 7.6 %all-to-all-start.2 = ((bf16[32,2,128,256]{3,1,2,0:T(2,128)(2,1)}), bf16[32,2,128,256]{3,1,2,0:T(2,128)(2,1)}, u32[]{:S(2)}, u32[]{:S(2)}) async-start(bf16[32,2,128,256]{3,1,2,0:T(2,128)(2,1)} %copy.64), calls=%async_computation.2 | async-start | bytes 8388608 | tf_op jit(solution)/shard_map/all_to_all | solution.py:59
  124.7 11.6 %reduce-scatter.5.cloned.1.call-start = ((), (), s32[]{:S(2)}) async-start(), calls=%async_computation.6 | async-start | bytes 6488064 | tf_op jit(solution)/shard_map/reduce_scatter | solution.py:86
  137.3 40.1 %all-to-all-done.2 = bf16[32,2,128,256]{3,1,2,0:T(2,128)(2,1)} async-done(((bf16[32,2,128,256]{3,1,2,0:T(2,128)(2,1)}), bf16[32,2,128,256]{3,1,2,0:T(2,128)(2,1)}, u32[]{:S(2)}, u32[]{:S(2)}) %all-to-all-start.2) | async-done | bytes 4194336 | tf_op jit(solution)/shard_map/all_to_all | solution.py:59
  177.5 8.9 %copy.65 = bf16[32,2,128,256]{3,1,0,2:T(2,128)(2,1)} copy(bf16[32,2,128,256]{3,1,2,0:T(2,128)(2,1)} %all-to-all-done.2) | data formatting | bytes 8388608 | tf_op jit(solution)/shard_map/all_to_all | solution.py:59
  186.3 7.2 %reshape.173 = bf16[64,128,256]{2,0,1:T(8,128)(2,1)} reshape(bf16[32,2,128,256]{3,1,0,2:T(2,128)(2,1)} %copy.65) | data formatting | bytes 8388608 | tf_op jit(solution)/shard_map/reshape | solution.py:67
  208.6 7.1 %gather_fusion = bf16[64,128,768]{2,1,0:T(8,128)(2,1)} fusion(bf16[8,128,768]{2,1,0:T(8,128)(2,1)S(1)} %bitcast.86, s32[1024]{0:T(1024)S(1)} %pad_clamp_fusion.3), kind=kCustom, calls=%fused_computation | custom fusion | bytes 25166080 | tf_op jit(solution)/shard_map/gather | solution.py:40
  215.7 6.8 %all-to-all-start = ((bf16[32,2,128,768]{3,2,1,0:T(8,128)(2,1)}), bf16[32,2,128,768]{3,2,1,0:T(8,128)(2,1)}, u32[]{:S(2)}, u32[]{:S(2)}) async-start(bf16[32,2,128,768]{3,2,1,0:T(8,128)(2,1)} %bitcast.90), calls=%async_computation | async-start | bytes 25165824 | tf_op jit(solution)/shard_map/all_to_all | solution.py:41
  233.9 10.9 %gather_fusion.1 = bf16[64,768,256]{2,1,0:T(8,128)(2,1)} fusion(bf16[5,768,256]{2,1,0:T(8,128)(2,1)S(1)} %bitcast.89, s32[1024]{0:T(1024)S(1)} %pad_clamp_fusion.2), kind=kCustom, calls=%fused_computation.1 | custom fusion | bytes 50331904 | tf_op jit(solution)/shard_map/gather | solution.py:39
  245.7 161.5 %reduce-scatter.5.cloned.1.call-done = f32[24,6,256]{2,1,0:T(8,128)} async-done(((f32[768,6,256]{2,1,0:T(8,128)}), f32[24,6,256]{2,1,0:T(8,128)}) %reduce-scatter.5.cloned.1.call-update) | async-done | bytes 147472 | tf_op jit(solution)/shard_map/reduce_scatter | solution.py:86
  408.4 38.7 %reduce-scatter.3.cloned.1.call-done = f32[256,768]{1,0:T(8,128)} async-done(((f32[1024,768]{1,0:T(8,128)}), f32[256,768]{1,0:T(8,128)}) %reduce-scatter.3.cloned.1.call-update) | async-done | bytes 786448 | tf_op jit(solution)/shard_map/reduce_scatter | solution.py:74
  449.0 67.3 %psum.14 = f32[5,4]{0,1:T(4,128)S(1)} all-reduce(f32[5,4]{0,1:T(4,128)S(1)} %convolution_bitcast_fusion.5), channel_id=1, replica_groups=mesh['shard'=32,'rep'=4] {'shard'}, use_global_device_ids=true, to_apply=%region_2.0 | all-reduce | flops 20 | bytes 160 | tf_op jit(solution)/shard_map/psum | solution.py:96
  519.7 9.3 %psum.15 = f32[5,4]{0,1:T(4,128)} all-reduce(f32[5,4]{0,1:T(4,128)S(1)} %psum.14), channel_id=1, replica_groups=mesh['shard'=32,'rep'=4] {'rep'}, use_global_device_ids=true, to_apply=%region_3.0 | all-reduce | flops 20 | bytes 160 | tf_op jit(solution)/shard_map/psum | solution.py:96
  529.0 15.7 %convolution_convert_fusion.2 = bf16[64,128,256]{2,1,0:T(8,128)(2,1)} fusion(bf16[64,128,768]{2,1,0:T(8,128)(2,1)} %bitcast.5, bf16[64,768,256]{2,1,0:T(8,128)(2,1)} %gather_fusion.1), kind=kOutput, calls=%fused_computation.12 | convolution fusion | flops 3223322624 | bytes 41943040 | tf_op jit(solution)/shard_map/snc,sco->sno/dot_general | solution.py:11
  544.7 12.0 %gather_fusion.2 = bf16[256,128,256]{2,1,0:T(8,128)(2,1)} fusion(bf16[64,128,256]{2,1,0:T(8,128)(2,1)} %convolution_convert_fusion.2, s32[1024]{0:T(1024)S(1)} %pad_clamp_fusion.1), kind=kCustom, calls=%fused_computation.2 | custom fusion | bytes 33555456 | tf_op jit(solution)/shard_map/gather | solution.py:43
  556.7 20.1 %convolution_bitcast_fusion.1 = f32[256,128,256]{1,2,0:T(8,128)} fusion(bf16[256,128,256]{2,1,0:T(8,128)(2,1)} %gather_fusion.2, bf16[1,256,128,128]{3,2,1,0:T(8,128)(2,1)} %param.18), kind=kOutput, calls=%fused_computation.6 | convolution fusion | flops 2147483648 | bytes 58720256 | tf_op jit(solution)/shard_map/tij,tjo->tio/dot_general | solution.py:44
  576.8 33.4 %copy.58 = f32[256,128,256]{2,0,1:T(8,128)} copy(f32[256,128,256]{1,2,0:T(8,128)} %convolution_bitcast_fusion.1) | data formatting | bytes 67108864 | tf_op jit(solution)/shard_map/tij,tjo->tio/dot_general | solution.py:44
  610.2 15.8 %fusion.14 = f32[8,128,256]{2,0,1:T(8,128)S(1)} fusion(f32[256,128,256]{2,0,1:T(8,128)} %copy.58, s32[256]{0:T(256)S(1)} %bitcast.98), kind=kOutput, calls=%fused_computation.35 | convolution fusion | flops 805308416 | bytes 34604032 | tf_op jit(solution)/shard_map/tb,tio->bio/dot_general | solution.py:46
  (71 shorter events, 38.5 us)
Async XLA Ops:
  7.2 129.4 %copy-start = (bf16[1024,768]{1,0:T(8,128)(2,1)S(1)}, bf16[1024,768]{1,0:T(8,128)(2,1)}, u32[]{:S(2)}) copy-start(bf16[1024,768]{1,0:T(8,128)(2,1)} %param.10) | copy-start | bytes 4718596
  8.7 108.4 %all-to-all-start.1 = ((s32[32,1,2]{2,1,0:T(1,128)}), s32[32,1,2]{2,1,0:T(1,128)S(1)}, u32[]{:S(2)}, u32[]{:S(2)}) async-start(s32[32,1,2]{2,1,0:T(1,128)} %copy.60), calls=%async_computation.1 | async-start | bytes 32768 | tf_op jit(solution)/shard_map/all_to_all | solution.py:34
  48.7 33.4 %copy-start.9 = (s32[1,256]{1,0:T(1,128)S(1)}, s32[1,256]{1,0:T(1,128)}, u32[]{:S(2)}) copy-start(s32[1,256]{1,0:T(1,128)} %param.16) | copy-start | bytes 3076
  117.1 19.3 %copy-start.11 = (s32[1,32,2]{1,2,0:T(2,128)S(1)}, s32[1,32,2]{1,2,0:T(2,128)}, u32[]{:S(2)}) copy-start(s32[1,32,2]{1,2,0:T(2,128)} %param.14) | copy-start | bytes 772
  117.1 19.5 %copy-start.1 = (bf16[1024,256]{1,0:T(8,128)(2,1)S(1)}, bf16[1024,256]{1,0:T(8,128)(2,1)}, u32[]{:S(2)}) copy-start(bf16[1024,256]{1,0:T(8,128)(2,1)} %param.19) | copy-start | bytes 1572868
  117.1 60.4 %all-to-all-start.2 = ((bf16[32,2,128,256]{3,1,2,0:T(2,128)(2,1)}), bf16[32,2,128,256]{3,1,2,0:T(2,128)(2,1)}, u32[]{:S(2)}, u32[]{:S(2)}) async-start(bf16[32,2,128,256]{3,1,2,0:T(2,128)(2,1)} %copy.64), calls=%async_computation.2 | async-start | bytes 8388608 | tf_op jit(solution)/shard_map/all_to_all | solution.py:59
  124.7 282.4 %reduce-scatter.5.cloned.1.call-start = ((), (), s32[]{:S(2)}) async-start(), calls=%async_computation.6 | async-start | bytes 6488064 | tf_op jit(solution)/shard_map/reduce_scatter | solution.py:86
  197.2 2.3 copy-start.4
  215.7 9.5 %copy-start.12 = (bf16[5,4]{0,1:T(4,128)(2,1)S(1)}, bf16[5,4]{0,1:T(4,128)(2,1)}, u32[]{:S(2)}) copy-start(bf16[5,4]{0,1:T(4,128)(2,1)} %param.12) | copy-start | bytes 124
  215.7 313.2 %all-to-all-start = ((bf16[32,2,128,768]{3,2,1,0:T(8,128)(2,1)}), bf16[32,2,128,768]{3,2,1,0:T(8,128)(2,1)}, u32[]{:S(2)}, u32[]{:S(2)}) async-start(bf16[32,2,128,768]{3,2,1,0:T(8,128)(2,1)} %bitcast.90), calls=%async_computation | async-start | bytes 25165824 | tf_op jit(solution)/shard_map/all_to_all | solution.py:41
  222.5 224.6 %reduce-scatter.3.cloned.1.call-start = ((), (), s32[]{:S(2)}) async-start(), calls=%async_computation.5 | async-start | bytes 3932160 | tf_op jit(solution)/shard_map/reduce_scatter | solution.py:74
  225.3 1.8 copy-start.5
  227.1 2.3 copy-start.2
  227.1 2.3 copy-start.6
  231.6 2.2 copy-start.3
  233.9 11.0 %copy-start.10 = (s32[1,256]{1,0:T(1,128)S(1)}, s32[1,256]{1,0:T(1,128)}, u32[]{:S(2)}) copy-start(s32[1,256]{1,0:T(1,128)} %param.16) | copy-start | bytes 3076
  233.9 282.4 %copy-start.13 = (bf16[5,4]{0,1:T(4,128)(2,1)S(1)}, bf16[5,4]{0,1:T(4,128)(2,1)}, u32[]{:S(2)}) copy-start(bf16[5,4]{0,1:T(4,128)(2,1)} %param.12) | copy-start | bytes 124
  576.8 33.4 %copy-start.8 = (s32[1,256]{1,0:T(1,128)S(1)}, s32[1,256]{1,0:T(1,128)}, u32[]{:S(2)}) copy-start(s32[1,256]{1,0:T(1,128)} %param.17) | copy-start | bytes 3076
  610.2 16.1 %copy-start.7 = (bf16[768,256]{1,0:T(8,128)(2,1)S(1)}, bf16[768,256]{1,0:T(8,128)(2,1)}, u32[]{:S(2)}) copy-start(bf16[768,256]{1,0:T(8,128)(2,1)} %param.13) | copy-start | bytes 1179652
Sparse Core Ops, SparseCore 0:
  208.5 198.5 reduce-scatter.4
  409.7 37.3 reduce-scatter.2
